TPU v7x, 512 devices: a whole 4x4x16 slice. The times are simulated.
512 devices in a mesh: tok: 64 (over y, z), head: 8 (over x, core).
Axes of the slice: x: 4, y: 4, z: 16, core: 2. Of those that a mesh axis runs over, the one named last changes fastest.
Arguments:
- source_keys: bfloat16 [16384, 2048], P('tok', 'head'), may hold values from -6 to 6
- source_values: bfloat16 [16384, 2048], P('tok', 'head'), may hold values from -6 to 6
- queries: bfloat16 [16384, 2048], P('tok', 'head'), may hold values from -6 to 6
- fast_weights: float32 [3, 16, 128, 512], P(None, 'head'), may hold values from -0.5 to 0.5
- step_size: float32 [16], P('head'), may hold values from 0.3 to 3
- edit_mask: int32 [64], P('tok'), may hold values 0 or 1
- out_proj: bfloat16 [2048, 2048], P(None, 'head'), may hold values from -0.125 to 0.125
Outputs:
- layer_out: bfloat16 [16384, 2048], P('tok', 'head')
Inputs may be any that keep to these rules, and one draw needn't show every extreme that they name: `edit_mask`: 1 marks a block of source frames whose keys and values update the fast weights, 0 a block of edited frames.
All inputs are finite; a program needn't handle non-finite values.
Results may differ from a plain program's by a relative error of at most 0.0087.
Values may be sent and summed in bfloat16 or wider, within the bound.
A program may use at most 64 MiB of HBM per device.

v0:
```python
import jax
import jax.numpy as jnp
from jax import lax
from jax.sharding import PartitionSpec as P

ITERS = 5


coef_a = 3.4445
coef_b = -4.775
coef_c = 2.0315
highest = lax.Precision.HIGHEST


def filled_up(lines, length):
    spare = -lines.shape[0] % length
    if not spare:
        return lines
    return jnp.concatenate([lines, jnp.zeros((spare, *lines.shape[1:]), lines.dtype)])


def from_everyone(shard, axis):
    length = lax.axis_size(axis)
    return lax.all_to_all(
        jnp.broadcast_to(shard[None], (length, *shard.shape)), axis, 0, 0, tiled=True
    )


def laid_out(pieces, dim):
    pieces = jnp.moveaxis(pieces, 0, dim)
    shape = pieces.shape
    return pieces.reshape(*shape[:dim], shape[dim] * shape[dim + 1], *shape[dim + 2 :])


def collect(shard, axis, dim):
    pieces = from_everyone(shard, axis)
    return laid_out(pieces, dim)


def split_up(shard, dim, length):
    shape = shard.shape
    pieces = shard.reshape(*shape[:dim], length, shape[dim] // length, *shape[dim + 1 :])
    return jnp.moveaxis(pieces, dim, 0)


def sent_and_summed(shard, axis, dim):
    length = lax.axis_size(axis)
    pieces = lax.all_to_all(split_up(shard, dim, length), axis, 0, 0, tiled=True)
    return jnp.sum(pieces, axis=0)


def nested_sum(shard, axes):
    lines = shard.reshape(-1, shard.shape[-1])
    padded = filled_up(lines, lax.axis_size(axes))
    whole = collect(sent_and_summed(padded, axes, 0), axes, 0)
    return lax.slice_in_dim(whole, 0, len(lines)).reshape(shard.shape)


def silu_grad(preact):
    sigmoid_value = jax.nn.sigmoid(preact)
    return sigmoid_value * (1.0 + preact * (1.0 - sigmoid_value))


def newton_steps(iterate, gram_matrix, gram_source):
    for sweeps in range(ITERS):
        if sweeps > 0:
            gram_matrix = gram_source(iterate)
        polynomial = coef_b * gram_matrix + coef_c * jnp.einsum(
            "...ij,...jk->...ik", gram_matrix, gram_matrix, precision=highest
        )
        iterate = coef_a * iterate + jnp.einsum(
            "...ij,...jf->...if", polynomial, iterate, precision=highest
        )
    return iterate


def local_gram(iterate):
    return jnp.einsum("...if,...jf->...ij", iterate, iterate, precision=highest)


def orthogonalize(gradients):
    scaling = lax.rsqrt(jnp.sum(gradients * gradients, axis=(-2, -1), keepdims=True) + 1e-06)
    iterate = gradients * scaling
    return newton_steps(iterate, local_gram(iterate), local_gram)


def renormalize(previous, proposed):
    old_norm = jnp.sqrt(jnp.sum(previous * previous, axis=-2, keepdims=True) + 1e-06)
    new_norm = jnp.sqrt(jnp.sum(proposed * proposed, axis=-2, keepdims=True) + 1e-06)
    return proposed * (old_norm / new_norm)


def on_device(source_keys, source_values, queries, fast_weights, step_size, edit_mask, out_proj):
    tok_rows = source_keys.shape[0]
    local_heads = fast_weights.shape[1]
    head_size = fast_weights.shape[2]
    blocks = edit_mask.shape[0]
    token_mask = jnp.repeat(edit_mask, tok_rows // blocks).astype(jnp.bfloat16)
    keys_heads = source_keys.reshape(tok_rows, local_heads, head_size)
    masked_values = (
        source_values.reshape(tok_rows, local_heads, head_size) * token_mask[:, None, None]
    )
    weights_low = fast_weights.astype(jnp.bfloat16)
    gate_pre = jnp.einsum(
        "thd,hdf->htf", keys_heads, weights_low[0], preferred_element_type=jnp.float32
    )
    up_pre = jnp.einsum(
        "thd,hdf->htf", keys_heads, weights_low[2], preferred_element_type=jnp.float32
    )
    hidden = (jax.nn.silu(gate_pre) * up_pre).astype(jnp.bfloat16)
    back_grad = jnp.einsum(
        "thd,hdf->htf", masked_values, weights_low[1], preferred_element_type=jnp.float32
    )
    gate_grad = (back_grad * up_pre * silu_grad(gate_pre)).astype(jnp.bfloat16)
    up_grad = (back_grad * jax.nn.silu(gate_pre)).astype(jnp.bfloat16)
    grad_gate = jnp.einsum(
        "thd,htf->hdf", keys_heads, gate_grad, preferred_element_type=jnp.float32
    )
    grad_down = jnp.einsum(
        "thd,htf->hdf", masked_values, hidden, preferred_element_type=jnp.float32
    )
    grad_up = jnp.einsum("thd,htf->hdf", keys_heads, up_grad, preferred_element_type=jnp.float32)
    partial_value = jnp.stack([grad_gate, grad_down, grad_up])
    head_rates = step_size[None, :, None, None]
    summed = nested_sum(partial_value, "tok")
    directions = orthogonalize(summed)
    updated = renormalize(fast_weights, fast_weights + head_rates * directions).astype(jnp.bfloat16)
    query_heads = queries.reshape(tok_rows, local_heads, head_size)
    read_gate = jnp.einsum(
        "thd,hdf->htf", query_heads, updated[0], preferred_element_type=jnp.float32
    )
    read_up = jnp.einsum(
        "thd,hdf->htf", query_heads, updated[2], preferred_element_type=jnp.float32
    )
    read_hidden = (jax.nn.silu(read_gate) * read_up).astype(jnp.bfloat16)
    read_out = jnp.einsum(
        "htf,hdf->thd", read_hidden, updated[1], preferred_element_type=jnp.float32
    )
    read_out = read_out.astype(jnp.bfloat16).reshape(tok_rows, local_heads * head_size)
    projected = jnp.dot(collect(read_out, "head", 1), out_proj, preferred_element_type=jnp.float32)
    return jax.nn.silu(projected).astype(jnp.bfloat16)


def solution(mesh):
    in_specs = (
        P("tok", "head"),
        P("tok", "head"),
        P("tok", "head"),
        P(None, "head", None, None),
        P("head"),
        P("tok"),
        P(None, "head"),
    )
    out_specs = P("tok", "head")
    return jax.shard_map(
        on_device, mesh=mesh, in_specs=in_specs, out_specs=out_specs, check_vma=False
    )
```

profile of v0, /device:TPU:1, one launch (start us, length us, event | category | flops | bytes accessed | tf_op | source)
XLA Modules:
  0.0 281.9 jit_solution(17054987807088991342)
XLA Ops:
  0.0 0.0 copy-start
  0.0 1.1 copy.30
  1.1 2.2 multiply_reduce_fusion.2
  3.3 0.0 copy-start.4
  3.3 0.3 fusion.21
  3.6 1.3 fusion.22
  5.7 0.1 copy.31
  5.8 0.3 fusion.23
  6.1 1.8 convolution_bitcast_fusion.4
  7.9 0.6 convolution_bitcast_fusion.3
  8.5 0.5 convolution_bitcast_fusion.2
  8.9 1.4 pad_maximum_fusion
  10.3 1.4 reshape_reshape.6
  11.8 113.9 %all_to_all.15 = f32[64,12,512]{2,1,0:T(8,128)} all-to-all(f32[64,12,512]{2,1,0:T(8,128)S(1)} %reshape_reshape.6), channel_id=1, replica_groups=mesh['tok'=64,'head'=8] {'tok'}, dimensions={0} | all-to-all | bytes 3145728 | tf_op jit(solution)/shard_map/all_to_all | solution.py:48
  125.6 1.7 reduce_sum.43
  127.4 0.2 broadcast_in_dim.6
  127.6 105.7 %all_to_all.16 = f32[64,12,512]{2,1,0:T(8,128)S(1)} all-to-all(f32[64,12,512]{2,1,0:T(8,128)S(1)} %broadcast_in_dim.6), channel_id=1, replica_groups=mesh['tok'=64,'head'=8] {'tok'}, dimensions={0} | all-to-all | bytes 3145728 | tf_op jit(solution)/shard_map/all_to_all | solution.py:24
  233.3 0.2 multiply_reduce_fusion
  233.5 0.1 reduce_sum.45
  233.7 0.1 reduce_sum.46
  233.7 1.3 reshape_reshape.7
  235.1 3.8 %fusion = f32[3,2,128,128]{3,2,1,0:T(8,128)S(1)} fusion(f32[3,2,128,512]{3,2,1,0:T(8,128)} %reshape_reshape.7, f32[3,2]{1,0:T(4,128)S(1)} %add_rsqrt_fusion), kind=kOutput, calls=%fused_computation.10 | convolution fusion | flops 604372992 | bytes 1966104 | tf_op jit(solution)/shard_map/...if,...jf->...ij/dot_general | solution.py:78
  238.9 0.5 fusion.10
  239.4 1.7 multiply_add_fusion.4
  241.1 1.6 fusion.36
  242.7 0.5 fusion.9
  243.2 1.5 multiply_add_fusion.3
  244.8 1.6 fusion.37
  246.3 0.5 fusion.8
  246.9 1.5 multiply_add_fusion.2
  248.4 1.8 fusion.38
  250.2 0.5 fusion.7
  250.8 1.5 multiply_add_fusion.1
  252.3 0.0 copy-start.2
  252.3 0.0 copy-start.6
  252.3 1.6 fusion.39
  253.9 0.5 fusion.6
  254.4 0.0 copy-done.2
  254.5 0.0 copy-done.6
  254.5 1.8 multiply_reduce_fusion.1
  256.2 0.0 copy-start.5
  256.3 0.2 multiply_convert_fusion
  256.5 0.6 copy-done.5
  257.2 0.3 convolution_bitcast_fusion.1
  257.4 0.5 fusion.11
  258.0 0.1 broadcast_in_dim.8
  258.1 22.7 %all_to_all.17 = bf16[8,256,256]{1,2,0:T(8,128)(2,1)S(1)} all-to-all(bf16[8,256,256]{1,2,0:T(8,128)(2,1)S(1)} %broadcast_in_dim.8), channel_id=1, replica_groups=mesh['tok'=64,'head'=8] {'head'}, dimensions={0} | all-to-all | bytes 2097152 | tf_op jit(solution)/shard_map/all_to_all | solution.py:24
  280.7 1.2 multiply_convert_fusion.7
  (9 shorter events, 0.1 us)
Async XLA Ops:
  0.0 280.7 %copy-start = (bf16[2048,256]{1,0:T(8,128)(2,1)S(1)}, bf16[2048,256]{1,0:T(8,128)(2,1)}, u32[]{:S(2)}) copy-start(bf16[2048,256]{1,0:T(8,128)(2,1)} %param.13) | copy-start | bytes 3145732
  3.3 2.4 copy-start.4
  6.1 1.8 copy-start.3
  235.1 4.3 %copy-start.1 = (f32[3,2,128,512]{3,2,1,0:T(8,128)S(1)}, f32[3,2,128,512]{3,2,1,0:T(8,128)}, u32[]{:S(2)}) copy-start(f32[3,2,128,512]{3,2,1,0:T(8,128)} %reshape_reshape.7) | copy-start | bytes 4718596
  252.3 2.2 copy-start.2
  252.3 2.2 copy-start.6
  256.2 0.9 copy-start.5
where the time goes:
time: 282 us
  blocking collectives  242 us (86%)
  matrix products  27.8 us (10%)
  other arithmetic  5.88 us (2%)
  local copies, waits for them, and re-layouts  5.08 us (2%)
    all_to_all x2, blocking collectives, from_everyone(): lax.all_to_all(jnp.broadcast_to(shard[None], (length, *shard.shape)), axi...  128 us
    all_to_all x1, blocking collectives, sent_and_summed(): lax.all_to_all(split_up(shard, dim, length), axis, 0, 0, tiled=True)  114 us
    dot_general x5, matrix products, local_gram(): return jnp.einsum('...if,...jf->...ij', iterate, iterate, precision=highest)  10.3 us
    dot_general x5, matrix products, newton_steps(): jnp.einsum('...ij,...jf->...if', polynomial, iterate, precision=highest)  7.99 us

commit v1 on v0

v1 whole, which is shorter than its diff:
```python
import jax
import jax.numpy as jnp
from jax import lax
from jax.experimental import pallas as pl
from jax.experimental.pallas import tpu as pltpu
from jax.sharding import PartitionSpec as P

ITERS = 5
NY = 4
NX = 4
WIN = 4

coef_a = 3.4445
coef_b = -4.775
coef_c = 2.0315

MESH = pl.DeviceIdType.MESH
F32 = jnp.float32
BF16 = jnp.bfloat16


def dot(a, b):
    return jnp.dot(a, b, preferred_element_type=F32)


def dot_nt(a, b):
    return lax.dot_general(a, b, (((1,), (1,)), ((), ())), preferred_element_type=F32)


def dot_tn(a, b):
    return lax.dot_general(a, b, (((0,), (0,)), ((), ())), preferred_element_type=F32)


def split(a):
    high = a.astype(BF16)
    return high, (a - high.astype(F32)).astype(BF16)


def newton_step(iterate):
    rows = iterate.shape[0]
    xh, xl = split(iterate)
    both = dot_nt(xh, jnp.concatenate([xh, xl], axis=0))
    cross = both[:, rows:]
    gram = both[:, :rows] + (cross + cross.T)
    ah, al = split(gram)
    both = dot(ah, jnp.concatenate([ah, al], axis=1))
    cross = both[:, rows:]
    square = both[:, :rows] + (cross + cross.T)
    ph, plo = split(coef_b * gram + coef_c * square)
    return coef_a * iterate + dot(
        jnp.concatenate([ph, plo, ph], axis=1), jnp.concatenate([xh, xh, xl], axis=0)
    )


def kernel(
    nz,
    keys, values, queries, weights, step, mask, proj,
    out,
    kbuf, vraw, vbuf, vother, qbuf, w, whalf, pj,
    acc, gb, rz1, rz2, sb, r4, gfull, xs, new, rf, r,
    lsem, p1s, p1r, p2s, p2r, p3s, p3r, p4s, p4r, fs, fr, xsnd, xrcv, cs, cr, e4, e8,
):
    t = lax.axis_index("tok")
    hd = lax.axis_index("head")
    y = t // nz
    z = t - y * nz
    x = hd // 2
    c = hd - 2 * x
    hs = y // 2
    ch = y - 2 * hs
    oh = 1 - hs
    pair = y + 1 - 2 * ch
    outer = NY - 1 - y
    diag = NY - 1 - pair
    i = lax.rem(z, WIN)

    def dev(yy, zz, xx, cc):
        return (yy * nz + zz, xx * 2 + cc)

    def zp(d):
        return lax.rem(z + d + nz, nz)

    def xp(d):
        return lax.rem(x + d + NX, NX)

    partner = dev(y, z, x, 1 - c)

    def send(src, dst, ss, rs, where):
        copy = pltpu.make_async_remote_copy(
            src_ref=src, dst_ref=dst, send_sem=ss, recv_sem=rs, device_id=where, device_id_type=MESH
        )
        copy.start()
        sent.append(copy)

    def arrived(dst, ss, rs):
        pltpu.make_async_remote_copy(
            src_ref=dst, dst_ref=dst, send_sem=ss, recv_sem=rs, device_id=partner, device_id_type=MESH
        ).wait_recv()

    sent = []

    def local(src, dst, k):
        copy = pltpu.make_async_copy(src, dst, lsem.at[k])
        copy.start()
        return copy

    def cols(a):
        return pl.ds(pl.multiple_of(a * 128, 128), 128)

    barrier = pltpu.get_barrier_semaphore()
    near = [dev(yy, z, x, c) for yy in (pair, outer, diag)]
    near += [dev(y, zp(d), x, c) for d in (1, -1, 2, -2)]
    near += [dev(y, z, xp(d), c) for d in (1, -1, 2)] + [partner]
    for peer in near:
        pl.semaphore_signal(barrier, inc=1, device_id=peer, device_id_type=MESH)

    v_in = [local(values.at[:, cols(hs)], vraw.at[0], 0), local(values.at[:, cols(oh)], vraw.at[1], 1)]
    k_in = local(keys.at[:, cols(hs)], kbuf.at[0], 2)
    wh_in = local(weights.at[:, hs, :, pl.ds(pl.multiple_of(ch * 256, 128), 256)], whalf, 3)
    w_in = local(weights.at[:, hs], w, 4)
    q_in = local(queries.at[:, cols(hs)], qbuf.at[0], 5)
    pj_in = local(proj, pj, 6)

    for copy in v_in:
        copy.wait()
    keep = mask[0].astype(F32)
    vbuf[0] = (vraw[0].astype(F32) * keep).astype(BF16)
    vother[...] = (vraw[1].astype(F32) * keep).astype(BF16)

    pl.semaphore_wait(barrier, len(near))
    to_pair, to_outer, to_diag = (dev(yy, z, x, c) for yy in (pair, outer, diag))
    send(keys.at[:, cols(oh)], kbuf.at[3], p1s.at[2], p1r.at[2], to_diag)
    send(vother, vbuf.at[3], p1s.at[5], p1r.at[5], to_diag)
    send(keys.at[:, cols(hs)], kbuf.at[1], p1s.at[0], p1r.at[0], to_pair)
    send(keys.at[:, cols(oh)], kbuf.at[2], p1s.at[1], p1r.at[1], to_outer)
    send(vbuf.at[0], vbuf.at[1], p1s.at[3], p1r.at[3], to_pair)
    send(vother, vbuf.at[2], p1s.at[4], p1r.at[4], to_outer)
    send(queries.at[:, cols(oh)], qbuf.at[1], p1s.at[6], p1r.at[6], to_outer)
    for d in (2, -2):
        pl.semaphore_signal(e4, inc=1, device_id=dev(y, zp(d), x, c), device_id_type=MESH)

    k_in.wait()
    wh_in.wait()
    low = [whalf[m].astype(BF16) for m in range(3)]
    for s in range(4):
        if s:
            arrived(kbuf.at[s], p1s.at[s - 1], p1r.at[s - 1])
            arrived(vbuf.at[s], p1s.at[s + 2], p1r.at[s + 2])
        k = kbuf[s]
        vm = vbuf[s]
        g = dot(k, low[0])
        u = dot(k, low[2])
        b = dot(vm, low[1])
        sig = jax.nn.sigmoid(g)
        silu = g * sig
        hid = (silu * u).astype(BF16)
        dg = (b * u * (sig * (1.0 + g * (1.0 - sig)))).astype(BF16)
        du = (b * silu).astype(BF16)
        terms = (dot_tn(k, dg), dot_tn(vm, hid), dot_tn(k, du))
        for m in range(3):
            acc[m] = terms[m] if s == 0 else acc[m] + terms[m]
        if s == 0:
            pl.semaphore_wait(e4, 2)
            for d in (4, -4):
                pl.semaphore_signal(e8, inc=1, device_id=dev(y, zp(d), x, c), device_id_type=MESH)

    for j in range(WIN):
        for half in range(2):
            for m in range(3):
                at = 32 * j + 16 * half
                gb[j, half, m] = acc[m, at : at + 16, :].astype(BF16)
    ahead, behind, across = (lax.rem(i + d, WIN) for d in (1, 3, 2))
    send(gb.at[across, 0], rz2.at[0], p2s.at[2], p2r.at[2], dev(y, zp(2), x, c))
    send(gb.at[across, 1], rz2.at[1], p2s.at[3], p2r.at[3], dev(y, zp(-2), x, c))
    send(gb.at[ahead], rz1.at[0], p2s.at[0], p2r.at[0], dev(y, zp(1), x, c))
    send(gb.at[behind], rz1.at[1], p2s.at[1], p2r.at[1], dev(y, zp(-1), x, c))
    for k in range(2):
        arrived(rz1.at[k], p2s.at[k], p2r.at[k])
    for k in range(2):
        arrived(rz2.at[k], p2s.at[2 + k], p2r.at[2 + k])
    sums = {}
    for half in range(2):
        for m in range(3):
            rows = pl.ds(pl.multiple_of(i * 32 + 16 * half, 16), 16)
            total = acc[m, rows, :] + rz1[0, half, m].astype(F32)
            total = total + rz1[1, half, m].astype(F32) + rz2[half, m].astype(F32)
            sums[half, m] = total
            sb[half, m] = total.astype(BF16)
    pl.semaphore_wait(e8, 2)
    send(sb, r4.at[2], p3s.at[2], p3r.at[2], dev(y, zp(8), x, c))
    send(sb, r4.at[0], p3s.at[0], p3r.at[0], dev(y, zp(4), x, c))
    send(sb, r4.at[1], p3s.at[1], p3r.at[1], dev(y, zp(-4), x, c))
    for k in range(3):
        arrived(r4.at[k], p3s.at[k], p3r.at[k])
    for half in range(2):
        for m in range(3):
            total = sums[half, m]
            for k in range(3):
                total = total + r4[k, half, m].astype(F32)
            gfull[ch, i, half, m] = total.astype(BF16)
    mine = gfull.at[ch, i]
    for base, yy in ((4, pair), (0, y)):
        send(gfull.at[ch, i, 0], gfull.at[ch, i, 0], p4s.at[base + 2], p4r.at[base + 2], dev(yy, zp(2), x, c))
        send(gfull.at[ch, i, 1], gfull.at[ch, i, 1], p4s.at[base + 3], p4r.at[base + 3], dev(yy, zp(-2), x, c))
        send(mine, mine, p4s.at[base], p4r.at[base], dev(yy, zp(1), x, c))
        send(mine, mine, p4s.at[base + 1], p4r.at[base + 1], dev(yy, zp(-1), x, c))
    send(mine, mine, p4s.at[8], p4r.at[8], dev(pair, z, x, c))

    w_in.wait()
    old = [jnp.sqrt(jnp.sum(w[m] * w[m], axis=0, keepdims=True) + 1e-06) for m in range(3)]

    arrived(gfull.at[1 - ch, i], p4s.at[8], p4r.at[8])
    for base, side in ((0, ch), (4, 1 - ch)):
        arrived(gfull.at[side, behind], p4s.at[base], p4r.at[base])
        arrived(gfull.at[side, ahead], p4s.at[base + 1], p4r.at[base + 1])
        arrived(gfull.at[side, across, 0], p4s.at[base + 2], p4r.at[base + 2])
        arrived(gfull.at[side, across, 1], p4s.at[base + 3], p4r.at[base + 3])

    for m in range(3):
        columns = [
            jnp.concatenate(
                [gfull[side, j, half, m] for j in range(WIN) for half in range(2)], axis=0
            )
            for side in range(2)
        ]
        grad = jnp.concatenate(columns, axis=1).astype(F32)
        xs[m] = grad * lax.rsqrt(jnp.sum(grad * grad, keepdims=True) + 1e-06)

    @pl.loop(0, ITERS)
    def _(_):
        for m in range(3):
            xs[m] = newton_step(xs[m])

    rate = step[hs]
    for m in range(3):
        proposed = w[m] + rate * xs[m]
        norm = jnp.sqrt(jnp.sum(proposed * proposed, axis=0, keepdims=True) + 1e-06)
        new[m] = (proposed * (old[m] / norm)).astype(BF16)

    def read_of(q):
        rg = dot(q, new[0])
        ru = dot(q, new[2])
        rh = (rg * jax.nn.sigmoid(rg) * ru).astype(BF16)
        return dot_nt(rh, new[1]).astype(BF16)

    around = (0, 1, -1, 2)
    own = 2 * hd + hs
    arrived(qbuf.at[1], p1s.at[6], p1r.at[6])
    rf[...] = read_of(qbuf[1])
    for k in (3, 1, 2, 0):
        send(rf, r.at[own], fs.at[k], fr.at[k], dev(outer, z, xp(around[k]), c))
    q_in.wait()
    r[own] = read_of(qbuf[0])
    for k in (3, 1, 2):
        send(r.at[own], r.at[own], xsnd.at[k - 1], xrcv.at[k - 1], dev(y, z, xp(around[k]), c))
    send(r.at[own], r.at[own], cs.at[0], cr.at[0], partner)
    pj_in.wait()

    def term(block):
        return dot(r[block], pj[pl.ds(pl.multiple_of(block * 128, 128), 128), :])

    def block_of(k, cc, head):
        return 2 * (2 * xp(-around[k]) + cc) + head

    total = term(own)
    for k in range(4):
        block = block_of(k, c, oh)
        arrived(r.at[block], fs.at[k], fr.at[k])
        send(r.at[block], r.at[block], cs.at[4 + k], cr.at[4 + k], partner)
        total = total + term(block)
    for k in range(1, 4):
        block = block_of(k, c, hs)
        arrived(r.at[block], xsnd.at[k - 1], xrcv.at[k - 1])
        send(r.at[block], r.at[block], cs.at[k], cr.at[k], partner)
        total = total + term(block)
    for k, head in [(0, hs)] + [(k, oh) for k in range(4)] + [(k, hs) for k in range(1, 4)]:
        slot = k if head is hs else 4 + k
        block = block_of(k, 1 - c, head)
        arrived(r.at[block], cs.at[slot], cr.at[slot])
        total = total + term(block)
    out[...] = (total * jax.nn.sigmoid(total)).astype(BF16)
    for copy in sent:
        copy.wait_send()


def on_device(nz, source_keys, source_values, queries, fast_weights, step_size, edit_mask, out_proj):
    rows, width = source_keys.shape
    dma = pltpu.SemaphoreType.DMA
    hbm = pl.BlockSpec(memory_space=pl.ANY)
    smem = pl.BlockSpec(memory_space=pltpu.SMEM)

    def body(*refs):
        kernel(nz, *refs)

    return pl.pallas_call(
        body,
        out_shape=jax.ShapeDtypeStruct((rows, width), BF16),
        in_specs=[hbm, hbm, hbm, hbm, smem, smem, hbm],
        out_specs=pl.BlockSpec(memory_space=pltpu.VMEM),
        scratch_shapes=[
            pltpu.VMEM((4, 256, 128), BF16),
            pltpu.VMEM((2, 256, 128), BF16),
            pltpu.VMEM((4, 256, 128), BF16),
            pltpu.VMEM((256, 128), BF16),
            pltpu.VMEM((2, 256, 128), BF16),
            pltpu.VMEM((3, 128, 512), F32),
            pltpu.VMEM((3, 128, 256), F32),
            pltpu.VMEM((2048, 256), BF16),
            pltpu.VMEM((3, 128, 256), F32),
            pltpu.VMEM((4, 2, 3, 16, 256), BF16),
            pltpu.VMEM((2, 2, 3, 16, 256), BF16),
            pltpu.VMEM((2, 3, 16, 256), BF16),
            pltpu.VMEM((2, 3, 16, 256), BF16),
            pltpu.VMEM((3, 2, 3, 16, 256), BF16),
            pltpu.VMEM((2, 4, 2, 3, 16, 256), BF16),
            pltpu.VMEM((3, 128, 512), F32),
            pltpu.VMEM((3, 128, 512), BF16),
            pltpu.VMEM((256, 128), BF16),
            pltpu.VMEM((16, 256, 128), BF16),
            dma((7,)), dma((7,)), dma((7,)), dma((4,)), dma((4,)), dma((3,)), dma((3,)),
            dma((9,)), dma((9,)), dma((4,)), dma((4,)), dma((3,)), dma((3,)), dma((8,)), dma((8,)),
            pltpu.SemaphoreType.REGULAR, pltpu.SemaphoreType.REGULAR,
        ],
        compiler_params=pltpu.CompilerParams(collective_id=0, has_side_effects=True),
        name="lact_step",
    )(source_keys, source_values, queries, fast_weights, step_size, edit_mask, out_proj)


def solution(mesh):
    nz = mesh.shape["tok"] // NY
    in_specs = (
        P("tok", "head"),
        P("tok", "head"),
        P("tok", "head"),
        P(None, "head", None, None),
        P("head"),
        P("tok"),
        P(None, "head"),
    )

    def device_step(*args):
        return on_device(nz, *args)

    return jax.shard_map(
        device_step, mesh=mesh, in_specs=in_specs, out_specs=P("tok", "head"), check_vma=False
    )
```

time: 282 us -> 65.3 us (0.23)
  blocking collectives: 242 us -> 0 us
  Pallas kernels: 0 us -> 62.9 us
  matrix products: 27.8 us -> 0 us
  other arithmetic: 5.88 us -> 0 us
  local copies, waits for them, and re-layouts: 5.08 us -> 1.57 us
    all_to_all x3 -> x0, blocking collectives: 242 us -> none  [the longest x2 128 us: from_everyone(): lax.all_to_all(jnp.broadcast_to(shard[None], (length, *shard.shape)), axi...]
    pallas_call x0 -> x1, Pallas kernels: none -> 62.9 us  [on_device(): pl.pallas_call(body, out_shape=jax.ShapeDtypeStruct((rows, width), BF16),...]
    dot_general x24 -> x0, matrix products: 27.8 us -> none  [the longest x5 10.3 us: local_gram(): return jnp.einsum('...if,...jf->...ij', iterate, iterate, precision=highest)]
    reduce_sum x4 -> x0, other arithmetic: 4.26 us -> none  [the longest x1 2.19 us: renormalize(): jnp.sum(previous * previous, axis=-2, keepdims=True) + 1e-06]
where the time goes in v1:
time: 65.3 us; the launch traced here: 65.1 us
  Pallas kernels  62.9 us (96%)
  local copies, waits for them, and re-layouts  1.57 us (2%)
  between operations  0.66 us (1%)
    pallas_call x1, Pallas kernels, on_device(): pl.pallas_call(body, out_shape=jax.ShapeDtypeStruct((rows, width), BF16),...  62.9 us
    unnamed x1, local copies, waits for them, and re-layouts  1.57 us

profile of v1, /device:TPU:1, one launch (start us, length us, event | category | flops | bytes accessed | tf_op | source)
XLA Modules:
  0.0 65.1 jit_solution(15379026218915046170)
XLA Ops:
  0.7 62.9 %lact_step.1 = bf16[256,256]{1,0:T(8,128)(2,1)} custom-call(bf16[256,256]{1,0:T(8,128)(2,1)} %refs_0_.1, bf16[256,256]{1,0:T(8,128)(2,1)} %refs_1_.1, bf16[256,256]{1,0:T(8,128)(2,1)} %refs_2_.1, f32[3,2,128,512]{3,2,1,0:T(8,128)} %refs_3_.1, f32[2]{0:T(128)} %refs_4_.1, s32[1]{0:T(128)S(6)} %copy.9.refs_5_, bf16[2048,256]{1,0:T(8,128)(2,1)} %refs_6_.1), custom_call_target="tpu_custom_call" | custom-call | tf_op jit(solution)/shard_map/lact_step/pallas_call | solution.py:295
  63.6 1.6 %copy.10 = bf16[256,256]{1,0:T(8,128)(2,1)} copy(bf16[256,256]{1,0:T(8,128)(2,1)} %lact_step.1) | data formatting | bytes 262144

commit v2 on v1

--- a/solution.py
+++ b/solution.py
@@ -36,20 +36,57 @@
     return high, (a - high.astype(F32)).astype(BF16)
 
 
-def newton_step(iterate):
-    rows = iterate.shape[0]
-    xh, xl = split(iterate)
-    both = dot_nt(xh, jnp.concatenate([xh, xl], axis=0))
-    cross = both[:, rows:]
-    gram = both[:, :rows] + (cross + cross.T)
-    ah, al = split(gram)
-    both = dot(ah, jnp.concatenate([ah, al], axis=1))
-    cross = both[:, rows:]
-    square = both[:, :rows] + (cross + cross.T)
-    ph, plo = split(coef_b * gram + coef_c * square)
-    return coef_a * iterate + dot(
-        jnp.concatenate([ph, plo, ph], axis=1), jnp.concatenate([xh, xh, xl], axis=0)
+def three(left, right):
+    return dot(
+        jnp.concatenate([left[0], left[1], left[0]], axis=1),
+        jnp.concatenate([right[0], right[0], right[1]], axis=0),
     )
+
+
+def orthogonalize(grads):
+    rows = grads[0].shape[0]
+    on_diagonal = lax.broadcasted_iota(jnp.int32, (rows, rows), 0) == lax.broadcasted_iota(
+        jnp.int32, (rows, rows), 1
+    )
+    eye = jnp.where(on_diagonal, coef_a, 0.0)
+    raw = [dot_nt(g, g) for g in grads]
+    scales = [
+        lax.rsqrt(jnp.sum(jnp.where(on_diagonal, gram, 0.0), keepdims=True) + 1e-06) for gram in raw
+    ]
+    grams = [gram * (scale * scale) for gram, scale in zip(raw, scales)]
+    factors = [None for _ in grads]
+    for sweep in range(ITERS):
+        halves = [split(gram) for gram in grams]
+        squares = [three(half, half) for half in halves]
+        polys = [
+            split(eye + coef_b * gram + coef_c * square) for gram, square in zip(grams, squares)
+        ]
+        if sweep == ITERS - 1:
+            return [
+                three(poly, split(moved)) * scale for poly, moved, scale in zip(polys, parts, scales)
+            ]
+        if sweep == 0:
+            products = [three(poly, half) for poly, half in zip(polys, halves)]
+            factors = polys
+        else:
+            both = [
+                three(
+                    poly,
+                    (
+                        jnp.concatenate([half[0], factor[0]], axis=1),
+                        jnp.concatenate([half[1], factor[1]], axis=1),
+                    ),
+                )
+                for poly, half, factor in zip(polys, halves, factors)
+            ]
+            products = [pair[:, :rows] for pair in both]
+            factors = [split(pair[:, rows:]) for pair in both]
+        grams = [three(split(product), poly) for product, poly in zip(products, polys)]
+        if sweep == ITERS - 2:
+            parts = [
+                dot(jnp.concatenate(factor, axis=1), jnp.concatenate([g, g], axis=0))
+                for factor, g in zip(factors, grads)
+            ]
 
 
 def kernel(
@@ -57,7 +94,7 @@
     keys, values, queries, weights, step, mask, proj,
     out,
     kbuf, vraw, vbuf, vother, qbuf, w, whalf, pj,
-    acc, gb, rz1, rz2, sb, r4, gfull, xs, new, rf, r,
+    acc, gb, rz1, rz2, sb, r4, gfull, new, rf, r,
     lsem, p1s, p1r, p2s, p2r, p3s, p3r, p4s, p4r, fs, fr, xsnd, xrcv, cs, cr, e4, e8,
 ):
     t = lax.axis_index("tok")
@@ -135,7 +172,6 @@
     send(keys.at[:, cols(oh)], kbuf.at[2], p1s.at[1], p1r.at[1], to_outer)
     send(vbuf.at[0], vbuf.at[1], p1s.at[3], p1r.at[3], to_pair)
     send(vother, vbuf.at[2], p1s.at[4], p1r.at[4], to_outer)
-    send(queries.at[:, cols(oh)], qbuf.at[1], p1s.at[6], p1r.at[6], to_outer)
     for d in (2, -2):
         pl.semaphore_signal(e4, inc=1, device_id=dev(y, zp(d), x, c), device_id_type=MESH)
 
@@ -164,76 +200,73 @@
             for d in (4, -4):
                 pl.semaphore_signal(e8, inc=1, device_id=dev(y, zp(d), x, c), device_id_type=MESH)
 
-    for j in range(WIN):
+    ahead, behind, across = (lax.rem(i + d, WIN) for d in (1, 3, 2))
+    for m in range(3):
+        for j in range(WIN):
+            for half in range(2):
+                at = 32 * j + 16 * half
+                gb[m, j, half] = acc[m, at : at + 16, :].astype(BF16)
+    for m in range(3):
+        send(gb.at[m, across, 0], rz2.at[m, 0], p2s.at[m, 2], p2r.at[m, 2], dev(y, zp(2), x, c))
+        send(gb.at[m, across, 1], rz2.at[m, 1], p2s.at[m, 3], p2r.at[m, 3], dev(y, zp(-2), x, c))
+        send(gb.at[m, ahead], rz1.at[m, 0], p2s.at[m, 0], p2r.at[m, 0], dev(y, zp(1), x, c))
+        send(gb.at[m, behind], rz1.at[m, 1], p2s.at[m, 1], p2r.at[m, 1], dev(y, zp(-1), x, c))
+    send(queries.at[:, cols(oh)], qbuf.at[1], p1s.at[6], p1r.at[6], to_outer)
+    pl.semaphore_wait(e8, 2)
+    sums = {}
+    for m in range(3):
+        for k in range(2):
+            arrived(rz1.at[m, k], p2s.at[m, k], p2r.at[m, k])
+        for k in range(2):
+            arrived(rz2.at[m, k], p2s.at[m, 2 + k], p2r.at[m, 2 + k])
         for half in range(2):
-            for m in range(3):
-                at = 32 * j + 16 * half
-                gb[j, half, m] = acc[m, at : at + 16, :].astype(BF16)
-    ahead, behind, across = (lax.rem(i + d, WIN) for d in (1, 3, 2))
-    send(gb.at[across, 0], rz2.at[0], p2s.at[2], p2r.at[2], dev(y, zp(2), x, c))
-    send(gb.at[across, 1], rz2.at[1], p2s.at[3], p2r.at[3], dev(y, zp(-2), x, c))
-    send(gb.at[ahead], rz1.at[0], p2s.at[0], p2r.at[0], dev(y, zp(1), x, c))
-    send(gb.at[behind], rz1.at[1], p2s.at[1], p2r.at[1], dev(y, zp(-1), x, c))
-    for k in range(2):
-        arrived(rz1.at[k], p2s.at[k], p2r.at[k])
-    for k in range(2):
-        arrived(rz2.at[k], p2s.at[2 + k], p2r.at[2 + k])
-    sums = {}
-    for half in range(2):
-        for m in range(3):
             rows = pl.ds(pl.multiple_of(i * 32 + 16 * half, 16), 16)
-            total = acc[m, rows, :] + rz1[0, half, m].astype(F32)
-            total = total + rz1[1, half, m].astype(F32) + rz2[half, m].astype(F32)
+            total = acc[m, rows, :] + rz1[m, 0, half].astype(F32)
+            total = total + rz1[m, 1, half].astype(F32) + rz2[m, half].astype(F32)
             sums[half, m] = total
-            sb[half, m] = total.astype(BF16)
-    pl.semaphore_wait(e8, 2)
-    send(sb, r4.at[2], p3s.at[2], p3r.at[2], dev(y, zp(8), x, c))
-    send(sb, r4.at[0], p3s.at[0], p3r.at[0], dev(y, zp(4), x, c))
-    send(sb, r4.at[1], p3s.at[1], p3r.at[1], dev(y, zp(-4), x, c))
-    for k in range(3):
-        arrived(r4.at[k], p3s.at[k], p3r.at[k])
-    for half in range(2):
-        for m in range(3):
+            sb[m, half] = total.astype(BF16)
+        send(sb.at[m], r4.at[m, 2], p3s.at[m, 2], p3r.at[m, 2], dev(y, zp(8), x, c))
+        send(sb.at[m], r4.at[m, 0], p3s.at[m, 0], p3r.at[m, 0], dev(y, zp(4), x, c))
+        send(sb.at[m], r4.at[m, 1], p3s.at[m, 1], p3r.at[m, 1], dev(y, zp(-4), x, c))
+    w_in.wait()
+    old = [jnp.sqrt(jnp.sum(w[m] * w[m], axis=0, keepdims=True) + 1e-06) for m in range(3)]
+    for m in range(3):
+        for k in range(3):
+            arrived(r4.at[m, k], p3s.at[m, k], p3r.at[m, k])
+        for half in range(2):
             total = sums[half, m]
             for k in range(3):
-                total = total + r4[k, half, m].astype(F32)
-            gfull[ch, i, half, m] = total.astype(BF16)
-    mine = gfull.at[ch, i]
-    for base, yy in ((4, pair), (0, y)):
-        send(gfull.at[ch, i, 0], gfull.at[ch, i, 0], p4s.at[base + 2], p4r.at[base + 2], dev(yy, zp(2), x, c))
-        send(gfull.at[ch, i, 1], gfull.at[ch, i, 1], p4s.at[base + 3], p4r.at[base + 3], dev(yy, zp(-2), x, c))
-        send(mine, mine, p4s.at[base], p4r.at[base], dev(yy, zp(1), x, c))
-        send(mine, mine, p4s.at[base + 1], p4r.at[base + 1], dev(yy, zp(-1), x, c))
-    send(mine, mine, p4s.at[8], p4r.at[8], dev(pair, z, x, c))
-
-    w_in.wait()
-    old = [jnp.sqrt(jnp.sum(w[m] * w[m], axis=0, keepdims=True) + 1e-06) for m in range(3)]
-
-    arrived(gfull.at[1 - ch, i], p4s.at[8], p4r.at[8])
-    for base, side in ((0, ch), (4, 1 - ch)):
-        arrived(gfull.at[side, behind], p4s.at[base], p4r.at[base])
-        arrived(gfull.at[side, ahead], p4s.at[base + 1], p4r.at[base + 1])
-        arrived(gfull.at[side, across, 0], p4s.at[base + 2], p4r.at[base + 2])
-        arrived(gfull.at[side, across, 1], p4s.at[base + 3], p4r.at[base + 3])
-
-    for m in range(3):
+                total = total + r4[m, k, half].astype(F32)
+            gfull[m, ch, i, half] = total.astype(BF16)
+        mine, first, second = gfull.at[m, ch, i], gfull.at[m, ch, i, 0], gfull.at[m, ch, i, 1]
+        for base, yy in ((4, pair), (0, y)):
+            ss, rs = p4s.at[m], p4r.at[m]
+            send(first, first, ss.at[base + 2], rs.at[base + 2], dev(yy, zp(2), x, c))
+            send(second, second, ss.at[base + 3], rs.at[base + 3], dev(yy, zp(-2), x, c))
+            send(mine, mine, ss.at[base], rs.at[base], dev(yy, zp(1), x, c))
+            send(mine, mine, ss.at[base + 1], rs.at[base + 1], dev(yy, zp(-1), x, c))
+        send(mine, mine, ss.at[8], rs.at[8], dev(pair, z, x, c))
+    grads = []
+    for m in range(3):
+        ss, rs = p4s.at[m], p4r.at[m]
+        arrived(gfull.at[m, 1 - ch, i], ss.at[8], rs.at[8])
+        for base, side in ((0, ch), (4, 1 - ch)):
+            arrived(gfull.at[m, side, behind], ss.at[base], rs.at[base])
+            arrived(gfull.at[m, side, ahead], ss.at[base + 1], rs.at[base + 1])
+            arrived(gfull.at[m, side, across, 0], ss.at[base + 2], rs.at[base + 2])
+            arrived(gfull.at[m, side, across, 1], ss.at[base + 3], rs.at[base + 3])
         columns = [
             jnp.concatenate(
-                [gfull[side, j, half, m] for j in range(WIN) for half in range(2)], axis=0
+                [gfull[m, side, j, half] for j in range(WIN) for half in range(2)], axis=0
             )
             for side in range(2)
         ]
-        grad = jnp.concatenate(columns, axis=1).astype(F32)
-        xs[m] = grad * lax.rsqrt(jnp.sum(grad * grad, keepdims=True) + 1e-06)
-
-    @pl.loop(0, ITERS)
-    def _(_):
-        for m in range(3):
-            xs[m] = newton_step(xs[m])
+        grads.append(jnp.concatenate(columns, axis=1))
+    directions = orthogonalize(grads)
 
     rate = step[hs]
     for m in range(3):
-        proposed = w[m] + rate * xs[m]
+        proposed = w[m] + rate * directions[m]
         norm = jnp.sqrt(jnp.sum(proposed * proposed, axis=0, keepdims=True) + 1e-06)
         new[m] = (proposed * (old[m] / norm)).astype(BF16)
 
@@ -307,18 +340,17 @@
             pltpu.VMEM((3, 128, 256), F32),
             pltpu.VMEM((2048, 256), BF16),
             pltpu.VMEM((3, 128, 256), F32),
-            pltpu.VMEM((4, 2, 3, 16, 256), BF16),
-            pltpu.VMEM((2, 2, 3, 16, 256), BF16),
-            pltpu.VMEM((2, 3, 16, 256), BF16),
-            pltpu.VMEM((2, 3, 16, 256), BF16),
-            pltpu.VMEM((3, 2, 3, 16, 256), BF16),
-            pltpu.VMEM((2, 4, 2, 3, 16, 256), BF16),
-            pltpu.VMEM((3, 128, 512), F32),
+            pltpu.VMEM((3, 4, 2, 16, 256), BF16),
+            pltpu.VMEM((3, 2, 2, 16, 256), BF16),
+            pltpu.VMEM((3, 2, 16, 256), BF16),
+            pltpu.VMEM((3, 2, 16, 256), BF16),
+            pltpu.VMEM((3, 3, 2, 16, 256), BF16),
+            pltpu.VMEM((3, 2, 4, 2, 16, 256), BF16),
             pltpu.VMEM((3, 128, 512), BF16),
             pltpu.VMEM((256, 128), BF16),
             pltpu.VMEM((16, 256, 128), BF16),
-            dma((7,)), dma((7,)), dma((7,)), dma((4,)), dma((4,)), dma((3,)), dma((3,)),
-            dma((9,)), dma((9,)), dma((4,)), dma((4,)), dma((3,)), dma((3,)), dma((8,)), dma((8,)),
+            dma((7,)), dma((7,)), dma((7,)), dma((3, 4)), dma((3, 4)), dma((3, 3)), dma((3, 3)),
+            dma((3, 9)), dma((3, 9)), dma((4,)), dma((4,)), dma((3,)), dma((3,)), dma((8,)), dma((8,)),
             pltpu.SemaphoreType.REGULAR, pltpu.SemaphoreType.REGULAR,
         ],
         compiler_params=pltpu.CompilerParams(collective_id=0, has_side_effects=True),

time: 65.3 us -> 60.6 us (0.928)
  Pallas kernels: 62.9 us -> 58.2 us
    pallas_call x1, Pallas kernels: 62.9 us -> 58.2 us  [on_device(): pl.pallas_call(body, out_shape=jax.ShapeDtypeStruct((rows, width), BF16),...]
where the time goes in v2:
time: 60.6 us; the launch traced here: 60.4 us
  Pallas kernels  58.2 us (96%)
  local copies, waits for them, and re-layouts  1.57 us (3%)
  between operations  0.66 us (1%)
    pallas_call x1, Pallas kernels, on_device(): pl.pallas_call(body, out_shape=jax.ShapeDtypeStruct((rows, width), BF16),...  58.2 us
    unnamed x1, local copies, waits for them, and re-layouts  1.57 us

profile of v2, /device:TPU:1, one launch (start us, length us, event | category | flops | bytes accessed | tf_op | source)
XLA Modules:
  0.0 60.4 jit_solution(13330493407964783852)
XLA Ops:
  0.7 58.2 %lact_step.1 = bf16[256,256]{1,0:T(8,128)(2,1)} custom-call(bf16[256,256]{1,0:T(8,128)(2,1)} %refs_0_.1, bf16[256,256]{1,0:T(8,128)(2,1)} %refs_1_.1, bf16[256,256]{1,0:T(8,128)(2,1)} %refs_2_.1, f32[3,2,128,512]{3,2,1,0:T(8,128)} %refs_3_.1, f32[2]{0:T(128)} %refs_4_.1, s32[1]{0:T(128)S(6)} %copy.9.refs_5_, bf16[2048,256]{1,0:T(8,128)(2,1)} %refs_6_.1), custom_call_target="tpu_custom_call" | custom-call | tf_op jit(solution)/shard_map/lact_step/pallas_call | solution.py:328
  58.8 1.6 %copy.10 = bf16[256,256]{1,0:T(8,128)(2,1)} copy(bf16[256,256]{1,0:T(8,128)(2,1)} %lact_step.1) | data formatting | bytes 262144

commit v3 on v2

--- a/solution.py
+++ b/solution.py
@@ -93,7 +93,7 @@
     nz,
     keys, values, queries, weights, step, mask, proj,
     out,
-    kbuf, vraw, vbuf, vother, qbuf, w, whalf, pj,
+    kbuf, vraw, vbuf, vother, qbuf, w, pj,
     acc, gb, rz1, rz2, sb, r4, gfull, new, rf, r,
     lsem, p1s, p1r, p2s, p2r, p3s, p3r, p4s, p4r, fs, fr, xsnd, xrcv, cs, cr, e4, e8,
 ):
@@ -108,7 +108,6 @@
     oh = 1 - hs
     pair = y + 1 - 2 * ch
     outer = NY - 1 - y
-    diag = NY - 1 - pair
     i = lax.rem(z, WIN)
 
     def dev(yy, zz, xx, cc):
@@ -145,45 +144,44 @@
         return pl.ds(pl.multiple_of(a * 128, 128), 128)
 
     barrier = pltpu.get_barrier_semaphore()
-    near = [dev(yy, z, x, c) for yy in (pair, outer, diag)]
-    near += [dev(y, zp(d), x, c) for d in (1, -1, 2, -2)]
-    near += [dev(y, z, xp(d), c) for d in (1, -1, 2)] + [partner]
+    shifts = (0, 1, -1, 2, -2)
+    to_outer = dev(outer, z, x, c)
+    near = [dev(pair, zp(d), x, c) for d in shifts] + [dev(y, zp(d), x, c) for d in shifts if d]
+    near += [dev(y, z, xp(d), c) for d in (1, -1, 2)] + [partner, to_outer]
     for peer in near:
         pl.semaphore_signal(barrier, inc=1, device_id=peer, device_id_type=MESH)
 
-    v_in = [local(values.at[:, cols(hs)], vraw.at[0], 0), local(values.at[:, cols(oh)], vraw.at[1], 1)]
+    v_out = local(values.at[:, cols(oh)], vraw.at[1], 0)
+    v_in = local(values.at[:, cols(hs)], vraw.at[0], 1)
     k_in = local(keys.at[:, cols(hs)], kbuf.at[0], 2)
-    wh_in = local(weights.at[:, hs, :, pl.ds(pl.multiple_of(ch * 256, 128), 256)], whalf, 3)
-    w_in = local(weights.at[:, hs], w, 4)
+    w_in = []
+    for side in range(2):
+        at = pl.ds(256 * side, 256)
+        w_in.append(local(weights.at[:, hs, :, at], w.at[side], 3 + side))
     q_in = local(queries.at[:, cols(hs)], qbuf.at[0], 5)
     pj_in = local(proj, pj, 6)
-
-    for copy in v_in:
-        copy.wait()
     keep = mask[0].astype(F32)
+    v_out.wait()
+    vother[...] = (vraw[1].astype(F32) * keep).astype(BF16)
+    v_in.wait()
     vbuf[0] = (vraw[0].astype(F32) * keep).astype(BF16)
-    vother[...] = (vraw[1].astype(F32) * keep).astype(BF16)
 
     pl.semaphore_wait(barrier, len(near))
-    to_pair, to_outer, to_diag = (dev(yy, z, x, c) for yy in (pair, outer, diag))
-    send(keys.at[:, cols(oh)], kbuf.at[3], p1s.at[2], p1r.at[2], to_diag)
-    send(vother, vbuf.at[3], p1s.at[5], p1r.at[5], to_diag)
-    send(keys.at[:, cols(hs)], kbuf.at[1], p1s.at[0], p1r.at[0], to_pair)
-    send(keys.at[:, cols(oh)], kbuf.at[2], p1s.at[1], p1r.at[1], to_outer)
-    send(vbuf.at[0], vbuf.at[1], p1s.at[3], p1r.at[3], to_pair)
-    send(vother, vbuf.at[2], p1s.at[4], p1r.at[4], to_outer)
+    send(keys.at[:, cols(oh)], kbuf.at[1], p1s.at[0], p1r.at[0], to_outer)
+    send(vother, vbuf.at[1], p1s.at[1], p1r.at[1], to_outer)
     for d in (2, -2):
         pl.semaphore_signal(e4, inc=1, device_id=dev(y, zp(d), x, c), device_id_type=MESH)
 
     k_in.wait()
-    wh_in.wait()
-    low = [whalf[m].astype(BF16) for m in range(3)]
-    for s in range(4):
-        if s:
-            arrived(kbuf.at[s], p1s.at[s - 1], p1r.at[s - 1])
-            arrived(vbuf.at[s], p1s.at[s + 2], p1r.at[s + 2])
-        k = kbuf[s]
-        vm = vbuf[s]
+    for copy in w_in:
+        copy.wait()
+    ahead, behind, across = (lax.rem(i + d, WIN) for d in (1, 3, 2))
+    halves = (ch, 1 - ch)
+
+    def gradients(block, side):
+        low = [w[side, m].astype(BF16) for m in range(3)]
+        k = kbuf[block]
+        vm = vbuf[block]
         g = dot(k, low[0])
         u = dot(k, low[2])
         b = dot(vm, low[1])
@@ -192,72 +190,89 @@
         hid = (silu * u).astype(BF16)
         dg = (b * u * (sig * (1.0 + g * (1.0 - sig)))).astype(BF16)
         du = (b * silu).astype(BF16)
-        terms = (dot_tn(k, dg), dot_tn(vm, hid), dot_tn(k, du))
+        return dot_tn(k, dg), dot_tn(vm, hid), dot_tn(k, du)
+
+    for dy in (1, 0):
+        terms = gradients(0, halves[dy])
         for m in range(3):
-            acc[m] = terms[m] if s == 0 else acc[m] + terms[m]
-        if s == 0:
-            pl.semaphore_wait(e4, 2)
-            for d in (4, -4):
-                pl.semaphore_signal(e8, inc=1, device_id=dev(y, zp(d), x, c), device_id_type=MESH)
-
-    ahead, behind, across = (lax.rem(i + d, WIN) for d in (1, 3, 2))
-    for m in range(3):
-        for j in range(WIN):
-            for half in range(2):
-                at = 32 * j + 16 * half
-                gb[m, j, half] = acc[m, at : at + 16, :].astype(BF16)
-    for m in range(3):
-        send(gb.at[m, across, 0], rz2.at[m, 0], p2s.at[m, 2], p2r.at[m, 2], dev(y, zp(2), x, c))
-        send(gb.at[m, across, 1], rz2.at[m, 1], p2s.at[m, 3], p2r.at[m, 3], dev(y, zp(-2), x, c))
-        send(gb.at[m, ahead], rz1.at[m, 0], p2s.at[m, 0], p2r.at[m, 0], dev(y, zp(1), x, c))
-        send(gb.at[m, behind], rz1.at[m, 1], p2s.at[m, 1], p2r.at[m, 1], dev(y, zp(-1), x, c))
-    send(queries.at[:, cols(oh)], qbuf.at[1], p1s.at[6], p1r.at[6], to_outer)
+            acc[dy, m] = terms[m]
+    pl.semaphore_wait(e4, 2)
+    for d in (4, -4):
+        pl.semaphore_signal(e8, inc=1, device_id=dev(y, zp(d), x, c), device_id_type=MESH)
+    for k in range(2):
+        arrived((kbuf, vbuf)[k].at[1], p1s.at[k], p1r.at[k])
+    for dy, yy in ((1, pair), (0, y)):
+        terms = gradients(1, halves[dy])
+        for m in range(3):
+            total = acc[dy, m] + terms[m]
+            if dy == 0:
+                acc[dy, m] = total
+            for j in range(WIN):
+                for half in range(2):
+                    at = 32 * j + 16 * half
+                    gb[dy, j, half, m] = total[at : at + 16, :].astype(BF16)
+        ss, rs = p2s.at[dy], p2r.at[dy]
+        send(gb.at[dy, across, 0], rz2.at[dy, 0], ss.at[3], rs.at[3], dev(yy, zp(2), x, c))
+        send(gb.at[dy, across, 1], rz2.at[dy, 1], ss.at[4], rs.at[4], dev(yy, zp(-2), x, c))
+        send(gb.at[dy, ahead], rz1.at[dy, 1], ss.at[1], rs.at[1], dev(yy, zp(1), x, c))
+        send(gb.at[dy, behind], rz1.at[dy, 2], ss.at[2], rs.at[2], dev(yy, zp(-1), x, c))
+        if dy:
+            send(gb.at[dy, i], rz1.at[dy, 0], ss.at[0], rs.at[0], dev(yy, z, x, c))
+    send(queries.at[:, cols(oh)], qbuf.at[1], p1s.at[2], p1r.at[2], to_outer)
     pl.semaphore_wait(e8, 2)
+    for dy in range(2):
+        ss, rs = p2s.at[dy], p2r.at[dy]
+        for k in range(3):
+            if dy or k:
+                arrived(rz1.at[dy, k], ss.at[k], rs.at[k])
+        for k in range(2):
+            arrived(rz2.at[dy, k], ss.at[3 + k], rs.at[3 + k])
     sums = {}
-    for m in range(3):
-        for k in range(2):
-            arrived(rz1.at[m, k], p2s.at[m, k], p2r.at[m, k])
-        for k in range(2):
-            arrived(rz2.at[m, k], p2s.at[m, 2 + k], p2r.at[m, 2 + k])
-        for half in range(2):
+    for half in range(2):
+        for m in range(3):
             rows = pl.ds(pl.multiple_of(i * 32 + 16 * half, 16), 16)
-            total = acc[m, rows, :] + rz1[m, 0, half].astype(F32)
-            total = total + rz1[m, 1, half].astype(F32) + rz2[m, half].astype(F32)
+            total = acc[0, m, rows, :]
+            for dy in range(2):
+                for k in range(3):
+                    if dy or k:
+                        total = total + rz1[dy, k, half, m].astype(F32)
+                total = total + rz2[dy, half, m].astype(F32)
             sums[half, m] = total
-            sb[m, half] = total.astype(BF16)
-        send(sb.at[m], r4.at[m, 2], p3s.at[m, 2], p3r.at[m, 2], dev(y, zp(8), x, c))
-        send(sb.at[m], r4.at[m, 0], p3s.at[m, 0], p3r.at[m, 0], dev(y, zp(4), x, c))
-        send(sb.at[m], r4.at[m, 1], p3s.at[m, 1], p3r.at[m, 1], dev(y, zp(-4), x, c))
-    w_in.wait()
-    old = [jnp.sqrt(jnp.sum(w[m] * w[m], axis=0, keepdims=True) + 1e-06) for m in range(3)]
-    for m in range(3):
-        for k in range(3):
-            arrived(r4.at[m, k], p3s.at[m, k], p3r.at[m, k])
-        for half in range(2):
+            sb[half, m] = total.astype(BF16)
+    send(sb, r4.at[2], p3s.at[2], p3r.at[2], dev(y, zp(8), x, c))
+    send(sb, r4.at[0], p3s.at[0], p3r.at[0], dev(y, zp(4), x, c))
+    send(sb, r4.at[1], p3s.at[1], p3r.at[1], dev(y, zp(-4), x, c))
+
+    def norms(a):
+        return jnp.sqrt(jnp.sum(a * a, axis=0, keepdims=True) + 1e-06)
+
+    old = [[norms(w[side, m]) for side in range(2)] for m in range(3)]
+    for k in range(3):
+        arrived(r4.at[k], p3s.at[k], p3r.at[k])
+    for half in range(2):
+        for m in range(3):
             total = sums[half, m]
             for k in range(3):
-                total = total + r4[m, k, half].astype(F32)
-            gfull[m, ch, i, half] = total.astype(BF16)
-        mine, first, second = gfull.at[m, ch, i], gfull.at[m, ch, i, 0], gfull.at[m, ch, i, 1]
-        for base, yy in ((4, pair), (0, y)):
-            ss, rs = p4s.at[m], p4r.at[m]
-            send(first, first, ss.at[base + 2], rs.at[base + 2], dev(yy, zp(2), x, c))
-            send(second, second, ss.at[base + 3], rs.at[base + 3], dev(yy, zp(-2), x, c))
-            send(mine, mine, ss.at[base], rs.at[base], dev(yy, zp(1), x, c))
-            send(mine, mine, ss.at[base + 1], rs.at[base + 1], dev(yy, zp(-1), x, c))
-        send(mine, mine, ss.at[8], rs.at[8], dev(pair, z, x, c))
+                total = total + r4[k, half, m].astype(F32)
+            gfull[ch, i, half, m] = total.astype(BF16)
+    mine, first, second = gfull.at[ch, i], gfull.at[ch, i, 0], gfull.at[ch, i, 1]
+    for base, yy in ((4, pair), (0, y)):
+        send(first, first, p4s.at[base + 2], p4r.at[base + 2], dev(yy, zp(2), x, c))
+        send(second, second, p4s.at[base + 3], p4r.at[base + 3], dev(yy, zp(-2), x, c))
+        send(mine, mine, p4s.at[base], p4r.at[base], dev(yy, zp(1), x, c))
+        send(mine, mine, p4s.at[base + 1], p4r.at[base + 1], dev(yy, zp(-1), x, c))
+    send(mine, mine, p4s.at[8], p4r.at[8], dev(pair, z, x, c))
+    arrived(gfull.at[1 - ch, i], p4s.at[8], p4r.at[8])
+    for base, side in ((0, ch), (4, 1 - ch)):
+        arrived(gfull.at[side, behind], p4s.at[base], p4r.at[base])
+        arrived(gfull.at[side, ahead], p4s.at[base + 1], p4r.at[base + 1])
+        arrived(gfull.at[side, across, 0], p4s.at[base + 2], p4r.at[base + 2])
+        arrived(gfull.at[side, across, 1], p4s.at[base + 3], p4r.at[base + 3])
     grads = []
     for m in range(3):
-        ss, rs = p4s.at[m], p4r.at[m]
-        arrived(gfull.at[m, 1 - ch, i], ss.at[8], rs.at[8])
-        for base, side in ((0, ch), (4, 1 - ch)):
-            arrived(gfull.at[m, side, behind], ss.at[base], rs.at[base])
-            arrived(gfull.at[m, side, ahead], ss.at[base + 1], rs.at[base + 1])
-            arrived(gfull.at[m, side, across, 0], ss.at[base + 2], rs.at[base + 2])
-            arrived(gfull.at[m, side, across, 1], ss.at[base + 3], rs.at[base + 3])
         columns = [
             jnp.concatenate(
-                [gfull[m, side, j, half] for j in range(WIN) for half in range(2)], axis=0
+                [gfull[side, j, half, m] for j in range(WIN) for half in range(2)], axis=0
             )
             for side in range(2)
         ]
@@ -266,9 +281,10 @@
 
     rate = step[hs]
     for m in range(3):
-        proposed = w[m] + rate * directions[m]
-        norm = jnp.sqrt(jnp.sum(proposed * proposed, axis=0, keepdims=True) + 1e-06)
-        new[m] = (proposed * (old[m] / norm)).astype(BF16)
+        for side in range(2):
+            at = slice(256 * side, 256 * side + 256)
+            proposed = w[side, m] + rate * directions[m][:, at]
+            new[m, :, at] = (proposed * (old[m][side] / norms(proposed))).astype(BF16)
 
     def read_of(q):
         rg = dot(q, new[0])
@@ -278,7 +294,7 @@
 
     around = (0, 1, -1, 2)
     own = 2 * hd + hs
-    arrived(qbuf.at[1], p1s.at[6], p1r.at[6])
+    arrived(qbuf.at[1], p1s.at[2], p1r.at[2])
     rf[...] = read_of(qbuf[1])
     for k in (3, 1, 2, 0):
         send(rf, r.at[own], fs.at[k], fr.at[k], dev(outer, z, xp(around[k]), c))
@@ -331,26 +347,25 @@
         in_specs=[hbm, hbm, hbm, hbm, smem, smem, hbm],
         out_specs=pl.BlockSpec(memory_space=pltpu.VMEM),
         scratch_shapes=[
-            pltpu.VMEM((4, 256, 128), BF16),
             pltpu.VMEM((2, 256, 128), BF16),
-            pltpu.VMEM((4, 256, 128), BF16),
+            pltpu.VMEM((2, 256, 128), BF16),
+            pltpu.VMEM((2, 256, 128), BF16),
             pltpu.VMEM((256, 128), BF16),
             pltpu.VMEM((2, 256, 128), BF16),
-            pltpu.VMEM((3, 128, 512), F32),
-            pltpu.VMEM((3, 128, 256), F32),
+            pltpu.VMEM((2, 3, 128, 256), F32),
             pltpu.VMEM((2048, 256), BF16),
-            pltpu.VMEM((3, 128, 256), F32),
-            pltpu.VMEM((3, 4, 2, 16, 256), BF16),
-            pltpu.VMEM((3, 2, 2, 16, 256), BF16),
-            pltpu.VMEM((3, 2, 16, 256), BF16),
-            pltpu.VMEM((3, 2, 16, 256), BF16),
-            pltpu.VMEM((3, 3, 2, 16, 256), BF16),
-            pltpu.VMEM((3, 2, 4, 2, 16, 256), BF16),
+            pltpu.VMEM((2, 3, 128, 256), F32),
+            pltpu.VMEM((2, 4, 2, 3, 16, 256), BF16),
+            pltpu.VMEM((2, 3, 2, 3, 16, 256), BF16),
+            pltpu.VMEM((2, 2, 3, 16, 256), BF16),
+            pltpu.VMEM((2, 3, 16, 256), BF16),
+            pltpu.VMEM((3, 2, 3, 16, 256), BF16),
+            pltpu.VMEM((2, 4, 2, 3, 16, 256), BF16),
             pltpu.VMEM((3, 128, 512), BF16),
             pltpu.VMEM((256, 128), BF16),
             pltpu.VMEM((16, 256, 128), BF16),
-            dma((7,)), dma((7,)), dma((7,)), dma((3, 4)), dma((3, 4)), dma((3, 3)), dma((3, 3)),
-            dma((3, 9)), dma((3, 9)), dma((4,)), dma((4,)), dma((3,)), dma((3,)), dma((8,)), dma((8,)),
+            dma((7,)), dma((3,)), dma((3,)), dma((2, 5)), dma((2, 5)), dma((3,)), dma((3,)),
+            dma((9,)), dma((9,)), dma((4,)), dma((4,)), dma((3,)), dma((3,)), dma((8,)), dma((8,)),
             pltpu.SemaphoreType.REGULAR, pltpu.SemaphoreType.REGULAR,
         ],
         compiler_params=pltpu.CompilerParams(collective_id=0, has_side_effects=True),

time: 60.6 us -> 57.9 us (0.955)
  Pallas kernels: 58.2 us -> 55.5 us
    pallas_call x1, Pallas kernels: 58.2 us -> 55.5 us  [on_device(): pl.pallas_call(body, out_shape=jax.ShapeDtypeStruct((rows, width), BF16),...]
where the time goes in v3:
time: 57.9 us; the launch traced here: 57.8 us
  Pallas kernels  55.5 us (96%)
  local copies, waits for them, and re-layouts  1.57 us (3%)
  between operations  0.66 us (1%)
    pallas_call x1, Pallas kernels, on_device(): pl.pallas_call(body, out_shape=jax.ShapeDtypeStruct((rows, width), BF16),...  55.5 us
    unnamed x1, local copies, waits for them, and re-layouts  1.57 us

profile of v3, /device:TPU:1, one launch (start us, length us, event | category | flops | bytes accessed | tf_op | source)
XLA Modules:
  0.0 57.8 jit_solution(14938940438275558860)
XLA Ops:
  0.7 55.5 %lact_step.1 = bf16[256,256]{1,0:T(8,128)(2,1)} custom-call(bf16[256,256]{1,0:T(8,128)(2,1)} %refs_0_.1, bf16[256,256]{1,0:T(8,128)(2,1)} %refs_1_.1, bf16[256,256]{1,0:T(8,128)(2,1)} %refs_2_.1, f32[3,2,128,512]{3,2,1,0:T(8,128)} %refs_3_.1, f32[2]{0:T(128)} %refs_4_.1, s32[1]{0:T(128)S(6)} %copy.9.refs_5_, bf16[2048,256]{1,0:T(8,128)(2,1)} %refs_6_.1), custom_call_target="tpu_custom_call" | custom-call | tf_op jit(solution)/shard_map/lact_step/pallas_call | solution.py:344
  56.2 1.6 %copy.10 = bf16[256,256]{1,0:T(8,128)(2,1)} copy(bf16[256,256]{1,0:T(8,128)(2,1)} %lact_step.1) | data formatting | bytes 262144

commit v4 on v3

--- a/solution.py
+++ b/solution.py
@@ -94,8 +94,8 @@
     keys, values, queries, weights, step, mask, proj,
     out,
     kbuf, vraw, vbuf, vother, qbuf, w, pj,
-    acc, gb, rz1, rz2, sb, r4, gfull, new, rf, r,
-    lsem, p1s, p1r, p2s, p2r, p3s, p3r, p4s, p4r, fs, fr, xsnd, xrcv, cs, cr, e4, e8,
+    flag, acc, gb, rz1, rz2, sb, r4, gfull, new, rf, r,
+    lsem, p1s, p1r, p2s, p2r, p3s, p3r, p4s, p4r, fs, fr, xsnd, xrcv, cs, cr, e2, e4, e8,
 ):
     t = lax.axis_index("tok")
     hd = lax.axis_index("head")
@@ -144,13 +144,14 @@
         return pl.ds(pl.multiple_of(a * 128, 128), 128)
 
     barrier = pltpu.get_barrier_semaphore()
-    shifts = (0, 1, -1, 2, -2)
     to_outer = dev(outer, z, x, c)
-    near = [dev(pair, zp(d), x, c) for d in shifts] + [dev(y, zp(d), x, c) for d in shifts if d]
-    near += [dev(y, z, xp(d), c) for d in (1, -1, 2)] + [partner, to_outer]
+    to_pair = dev(pair, z, x, c)
+    beside = [dev(y, zp(d), x, c) for d in (1, -1)] + [dev(y, z, xp(d), c) for d in (1, -1)]
+    near = beside + [to_outer, to_pair, partner]
     for peer in near:
         pl.semaphore_signal(barrier, inc=1, device_id=peer, device_id_type=MESH)
 
+    mask_in = local(mask, flag, 7)
     v_out = local(values.at[:, cols(oh)], vraw.at[1], 0)
     v_in = local(values.at[:, cols(hs)], vraw.at[0], 1)
     k_in = local(keys.at[:, cols(hs)], kbuf.at[0], 2)
@@ -160,7 +161,8 @@
         w_in.append(local(weights.at[:, hs, :, at], w.at[side], 3 + side))
     q_in = local(queries.at[:, cols(hs)], qbuf.at[0], 5)
     pj_in = local(proj, pj, 6)
-    keep = mask[0].astype(F32)
+    mask_in.wait()
+    keep = flag[0].astype(F32)
     v_out.wait()
     vother[...] = (vraw[1].astype(F32) * keep).astype(BF16)
     v_in.wait()
@@ -169,8 +171,11 @@
     pl.semaphore_wait(barrier, len(near))
     send(keys.at[:, cols(oh)], kbuf.at[1], p1s.at[0], p1r.at[0], to_outer)
     send(vother, vbuf.at[1], p1s.at[1], p1r.at[1], to_outer)
-    for d in (2, -2):
-        pl.semaphore_signal(e4, inc=1, device_id=dev(y, zp(d), x, c), device_id_type=MESH)
+    def tell(sem, peers):
+        for peer in peers:
+            pl.semaphore_signal(sem, inc=1, device_id=peer, device_id_type=MESH)
+
+    tell(e2, beside)
 
     k_in.wait()
     for copy in w_in:
@@ -196,9 +201,11 @@
         terms = gradients(0, halves[dy])
         for m in range(3):
             acc[dy, m] = terms[m]
-    pl.semaphore_wait(e4, 2)
-    for d in (4, -4):
-        pl.semaphore_signal(e8, inc=1, device_id=dev(y, zp(d), x, c), device_id_type=MESH)
+        if dy:
+            pl.semaphore_wait(e2, len(beside))
+            tell(e4, [dev(y, zp(d), x, c) for d in (2, -2)] + [to_pair, to_outer])
+    pl.semaphore_wait(e4, 4)
+    tell(e8, [dev(y, zp(d), x, c) for d in (4, -4)])
     for k in range(2):
         arrived((kbuf, vbuf)[k].at[1], p1s.at[k], p1r.at[k])
     for dy, yy in ((1, pair), (0, y)):
@@ -311,20 +318,21 @@
     def block_of(k, cc, head):
         return 2 * (2 * xp(-around[k]) + cc) + head
 
+    coming = [(0, 0), (1, 1), (1, 2), (0, 1), (0, 2), (1, 3), (0, 3)]
+    for line, k in coming:
+        block = block_of(k, c, (oh, hs)[line])
+        if line:
+            arrived(r.at[block], xsnd.at[k - 1], xrcv.at[k - 1])
+        else:
+            arrived(r.at[block], fs.at[k], fr.at[k])
+        slot = k if line else 4 + k
+        send(r.at[block], r.at[block], cs.at[slot], cr.at[slot], partner)
     total = term(own)
-    for k in range(4):
-        block = block_of(k, c, oh)
-        arrived(r.at[block], fs.at[k], fr.at[k])
-        send(r.at[block], r.at[block], cs.at[4 + k], cr.at[4 + k], partner)
-        total = total + term(block)
-    for k in range(1, 4):
-        block = block_of(k, c, hs)
-        arrived(r.at[block], xsnd.at[k - 1], xrcv.at[k - 1])
-        send(r.at[block], r.at[block], cs.at[k], cr.at[k], partner)
-        total = total + term(block)
-    for k, head in [(0, hs)] + [(k, oh) for k in range(4)] + [(k, hs) for k in range(1, 4)]:
-        slot = k if head is hs else 4 + k
-        block = block_of(k, 1 - c, head)
+    for line, k in coming:
+        total = total + term(block_of(k, c, (oh, hs)[line]))
+    for line, k in [(1, 0)] + coming:
+        slot = k if line else 4 + k
+        block = block_of(k, 1 - c, (oh, hs)[line])
         arrived(r.at[block], cs.at[slot], cr.at[slot])
         total = total + term(block)
     out[...] = (total * jax.nn.sigmoid(total)).astype(BF16)
@@ -343,8 +351,8 @@
 
     return pl.pallas_call(
         body,
-        out_shape=jax.ShapeDtypeStruct((rows, width), BF16),
-        in_specs=[hbm, hbm, hbm, hbm, smem, smem, hbm],
+        out_shape=pltpu.VMEM((rows, width), BF16),
+        in_specs=[hbm, hbm, hbm, hbm, smem, pl.BlockSpec(memory_space=pltpu.HBM), hbm],
         out_specs=pl.BlockSpec(memory_space=pltpu.VMEM),
         scratch_shapes=[
             pltpu.VMEM((2, 256, 128), BF16),
@@ -354,6 +362,7 @@
             pltpu.VMEM((2, 256, 128), BF16),
             pltpu.VMEM((2, 3, 128, 256), F32),
             pltpu.VMEM((2048, 256), BF16),
+            pltpu.SMEM((1,), jnp.int32),
             pltpu.VMEM((2, 3, 128, 256), F32),
             pltpu.VMEM((2, 4, 2, 3, 16, 256), BF16),
             pltpu.VMEM((2, 3, 2, 3, 16, 256), BF16),
@@ -364,9 +373,9 @@
             pltpu.VMEM((3, 128, 512), BF16),
             pltpu.VMEM((256, 128), BF16),
             pltpu.VMEM((16, 256, 128), BF16),
-            dma((7,)), dma((3,)), dma((3,)), dma((2, 5)), dma((2, 5)), dma((3,)), dma((3,)),
+            dma((8,)), dma((3,)), dma((3,)), dma((2, 5)), dma((2, 5)), dma((3,)), dma((3,)),
             dma((9,)), dma((9,)), dma((4,)), dma((4,)), dma((3,)), dma((3,)), dma((8,)), dma((8,)),
-            pltpu.SemaphoreType.REGULAR, pltpu.SemaphoreType.REGULAR,
+            pltpu.SemaphoreType.REGULAR, pltpu.SemaphoreType.REGULAR, pltpu.SemaphoreType.REGULAR,
         ],
         compiler_params=pltpu.CompilerParams(collective_id=0, has_side_effects=True),
         name="lact_step",

time: 57.9 us -> 56.5 us (0.976)
  local copies, waits for them, and re-layouts: 1.57 us -> 0.66 us
    unnamed x1, local copies, waits for them, and re-layouts: 1.57 us -> 0.66 us
where the time goes in v4:
time: 56.5 us; the launch traced here: 56.3 us
  Pallas kernels  55 us (97%)
  local copies, waits for them, and re-layouts  0.66 us (1%)
  between operations  0.66 us (1%)
    pallas_call x1, Pallas kernels, on_device(): pl.pallas_call(body, out_shape=pltpu.VMEM((rows, width), BF16), in_specs=...  55 us

profile of v4, /device:TPU:1, one launch (start us, length us, event | category | flops | bytes accessed | tf_op | source)
XLA Modules:
  0.0 56.3 jit_solution(1310278170989645095)
XLA Ops:
  0.7 55.0 %lact_step.1 = bf16[256,256]{1,0:T(8,128)(2,1)S(1)} custom-call(bf16[256,256]{1,0:T(8,128)(2,1)} %refs_0_.1, bf16[256,256]{1,0:T(8,128)(2,1)} %refs_1_.1, bf16[256,256]{1,0:T(8,128)(2,1)} %refs_2_.1, f32[3,2,128,512]{3,2,1,0:T(8,128)} %refs_3_.1, f32[2]{0:T(128)} %refs_4_.1, s32[1]{0:T(128)S(6)} %copy.10.refs_5_, bf16[2048,256]{1,0:T(8,128)(2,1)} %refs_6_.1), custom_call_target="tpu_custom_call" | custom-call | tf_op jit(solution)/shard_map/lact_step/pallas_call | solution.py:352
  55.7 0.7 %copy.9 = bf16[256,256]{1,0:T(8,128)(2,1)} copy(bf16[256,256]{1,0:T(8,128)(2,1)S(1)} %lact_step.1) | data formatting | bytes 262144

commit v5 on v4

--- a/solution.py
+++ b/solution.py
@@ -247,6 +247,7 @@
             sums[half, m] = total
             sb[half, m] = total.astype(BF16)
     send(sb, r4.at[2], p3s.at[2], p3r.at[2], dev(y, zp(8), x, c))
+    sent.pop().wait_send()
     send(sb, r4.at[0], p3s.at[0], p3r.at[0], dev(y, zp(4), x, c))
     send(sb, r4.at[1], p3s.at[1], p3r.at[1], dev(y, zp(-4), x, c))
 
@@ -302,9 +303,12 @@
     around = (0, 1, -1, 2)
     own = 2 * hd + hs
     arrived(qbuf.at[1], p1s.at[2], p1r.at[2])
-    rf[...] = read_of(qbuf[1])
-    for k in (3, 1, 2, 0):
-        send(rf, r.at[own], fs.at[k], fr.at[k], dev(outer, z, xp(around[k]), c))
+    for half in range(2):
+        part = pl.ds(128 * half, 128)
+        rf[part, :] = read_of(qbuf[1, part, :])
+        for k in (3, 1, 2, 0):
+            where = dev(outer, z, xp(around[k]), c)
+            send(rf.at[part], r.at[own, part], fs.at[k, half], fr.at[k, half], where)
     q_in.wait()
     r[own] = read_of(qbuf[0])
     for k in (3, 1, 2):
@@ -324,7 +328,8 @@
         if line:
             arrived(r.at[block], xsnd.at[k - 1], xrcv.at[k - 1])
         else:
-            arrived(r.at[block], fs.at[k], fr.at[k])
+            for half in range(2):
+                arrived(r.at[block, pl.ds(128 * half, 128)], fs.at[k, half], fr.at[k, half])
         slot = k if line else 4 + k
         send(r.at[block], r.at[block], cs.at[slot], cr.at[slot], partner)
     total = term(own)
@@ -374,7 +379,7 @@
             pltpu.VMEM((256, 128), BF16),
             pltpu.VMEM((16, 256, 128), BF16),
             dma((8,)), dma((3,)), dma((3,)), dma((2, 5)), dma((2, 5)), dma((3,)), dma((3,)),
-            dma((9,)), dma((9,)), dma((4,)), dma((4,)), dma((3,)), dma((3,)), dma((8,)), dma((8,)),
+            dma((9,)), dma((9,)), dma((4, 2)), dma((4, 2)), dma((3,)), dma((3,)), dma((8,)), dma((8,)),
             pltpu.SemaphoreType.REGULAR, pltpu.SemaphoreType.REGULAR, pltpu.SemaphoreType.REGULAR,
         ],
         compiler_params=pltpu.CompilerParams(collective_id=0, has_side_effects=True),

time: 56.5 us -> 56.5 us (level)
  no operation moved by 1% of the time
where the time goes in v5:
time: 56.5 us; the launch traced here: 56.4 us
  Pallas kernels  55 us (97%)
  local copies, waits for them, and re-layouts  0.66 us (1%)
  between operations  0.66 us (1%)
    pallas_call x1, Pallas kernels, on_device(): pl.pallas_call(body, out_shape=pltpu.VMEM((rows, width), BF16), in_specs=...  55 us

profile of v5, /device:TPU:1, one launch (start us, length us, event | category | flops | bytes accessed | tf_op | source)
XLA Modules:
  0.0 56.4 jit_solution(700884416908811413)
XLA Ops:
  0.7 55.0 %lact_step.1 = bf16[256,256]{1,0:T(8,128)(2,1)S(1)} custom-call(bf16[256,256]{1,0:T(8,128)(2,1)} %refs_0_.1, bf16[256,256]{1,0:T(8,128)(2,1)} %refs_1_.1, bf16[256,256]{1,0:T(8,128)(2,1)} %refs_2_.1, f32[3,2,128,512]{3,2,1,0:T(8,128)} %refs_3_.1, f32[2]{0:T(128)} %refs_4_.1, s32[1]{0:T(128)S(6)} %copy.10.refs_5_, bf16[2048,256]{1,0:T(8,128)(2,1)} %refs_6_.1), custom_call_target="tpu_custom_call" | custom-call | tf_op jit(solution)/shard_map/lact_step/pallas_call | solution.py:357
  55.7 0.7 %copy.9 = bf16[256,256]{1,0:T(8,128)(2,1)} copy(bf16[256,256]{1,0:T(8,128)(2,1)S(1)} %lact_step.1) | data formatting | bytes 262144

commit v6 on v5

--- a/solution.py
+++ b/solution.py
@@ -306,9 +306,12 @@
     for half in range(2):
         part = pl.ds(128 * half, 128)
         rf[part, :] = read_of(qbuf[1, part, :])
-        for k in (3, 1, 2, 0):
+        for k in (3, 1, 2):
             where = dev(outer, z, xp(around[k]), c)
             send(rf.at[part], r.at[own, part], fs.at[k, half], fr.at[k, half], where)
+    for half in range(2):
+        part = pl.ds(128 * half, 128)
+        send(rf.at[part], r.at[own, part], fs.at[0, half], fr.at[0, half], to_outer)
     q_in.wait()
     r[own] = read_of(qbuf[0])
     for k in (3, 1, 2):

time: 56.5 us -> 56.5 us (level)
  no operation moved by 1% of the time
where the time goes in v6:
time: 56.5 us; the launch traced here: 56.4 us
  Pallas kernels  55 us (97%)
  local copies, waits for them, and re-layouts  0.66 us (1%)
  between operations  0.66 us (1%)
    pallas_call x1, Pallas kernels, on_device(): pl.pallas_call(body, out_shape=pltpu.VMEM((rows, width), BF16), in_specs=...  55 us

profile of v6, /device:TPU:1, one launch (start us, length us, event | category | flops | bytes accessed | tf_op | source)
XLA Modules:
  0.0 56.4 jit_solution(16716580998399230752)
XLA Ops:
  0.7 55.0 %lact_step.1 = bf16[256,256]{1,0:T(8,128)(2,1)S(1)} custom-call(bf16[256,256]{1,0:T(8,128)(2,1)} %refs_0_.1, bf16[256,256]{1,0:T(8,128)(2,1)} %refs_1_.1, bf16[256,256]{1,0:T(8,128)(2,1)} %refs_2_.1, f32[3,2,128,512]{3,2,1,0:T(8,128)} %refs_3_.1, f32[2]{0:T(128)} %refs_4_.1, s32[1]{0:T(128)S(6)} %copy.10.refs_5_, bf16[2048,256]{1,0:T(8,128)(2,1)} %refs_6_.1), custom_call_target="tpu_custom_call" | custom-call | tf_op jit(solution)/shard_map/lact_step/pallas_call | solution.py:360
  55.7 0.7 %copy.9 = bf16[256,256]{1,0:T(8,128)(2,1)} copy(bf16[256,256]{1,0:T(8,128)(2,1)S(1)} %lact_step.1) | data formatting | bytes 262144
